TPU v7x, 256 devices: a whole 4x4x8 slice. The times are simulated.
256 devices in a mesh: space: 32 (over z, x), sample: 8 (over y, core).
Axes of the slice: x: 4, y: 4, z: 8, core: 2. Of those that a mesh axis runs over, the one named last changes fastest.
Arguments:
- crops: bfloat16 [256, 16, 64, 1024], P('sample', None, 'space'), may hold values from -6 to 6
- first_kernel: bfloat16 [32, 16, 3, 3, 3], replicated, may hold values from -0.3125 to 0.3125
- second_kernel: bfloat16 [64, 32, 3, 3, 3], replicated, may hold values from -0.21875 to 0.21875
- out_grad: bfloat16 [256, 64, 16, 64], P(('sample', 'space')), may hold values from -0.03125 to 0.03125
Outputs:
- features_out: bfloat16 [256, 64, 16, 64], P(('sample', 'space'))
- first_grad: float32 [32, 16, 3, 3, 3], replicated
- second_grad: float32 [64, 32, 3, 3, 3], replicated
All inputs are finite; a program needn't handle non-finite values.
Results may differ from a plain program's by a relative error of at most 0.012.
Values may be sent and summed in bfloat16 or wider, within the bound.
A program may use at most 128 MiB of HBM per device.

v0:
```python
import jax
import jax.numpy as jnp
from jax import lax
from jax.sharding import PartitionSpec as P

HEIGHT = 8
WIDTH = 128


def forward_conv(field, kernel, depth_pad):
    return lax.conv_general_dilated(
        field,
        kernel,
        (2, 2, 2),
        (depth_pad, (1, 0), (1, 0)),
        dimension_numbers=("NCDHW", "OIDHW", "NCDHW"),
        preferred_element_type=jnp.float32,
    )


def kernel_grad(field, cotangent, depth_pad):
    return lax.conv_general_dilated(
        field,
        cotangent,
        (1, 1, 1),
        (depth_pad, (1, 0), (1, 0)),
        rhs_dilation=(2, 2, 2),
        dimension_numbers=("CNDHW", "IODHW", "CNDHW"),
        preferred_element_type=jnp.float32,
    )


def input_grad(cotangent, kernel):
    flipped = kernel[:, :, ::-1, ::-1, ::-1]
    return lax.conv_general_dilated(
        cotangent,
        flipped,
        (1, 1, 1),
        ((1, 2), (1, 2), (1, 2)),
        lhs_dilation=(2, 2, 2),
        dimension_numbers=("NCDHW", "IODHW", "NCDHW"),
        preferred_element_type=jnp.float32,
    )


def silu_slope(value):
    sigma = jax.nn.sigmoid(value)
    return sigma * (1.0 + value * (1.0 - sigma))


def body(crops, first_kernel, second_kernel, out_grad):
    local_samples, channels_in, planes, flat_cells = crops.shape
    whole_input = lax.all_to_all(crops, "space", split_axis=0, concat_axis=2, tiled=True)
    whole_input = whole_input.reshape(
        whole_input.shape[0], channels_in, whole_input.shape[2], HEIGHT, WIDTH
    )
    first_pre = forward_conv(whole_input, first_kernel, (1, 0))
    act_whole = jax.nn.silu(first_pre).astype(jnp.bfloat16)
    sample_count = act_whole.shape[0]
    second_pre = forward_conv(act_whole, second_kernel, (1, 0))
    features_out = second_pre.astype(jnp.bfloat16).reshape(out_grad.shape)
    cotangent = out_grad.reshape(
        sample_count, out_grad.shape[1], out_grad.shape[2], HEIGHT // 4, WIDTH // 4
    )
    second_grad = kernel_grad(act_whole, cotangent, (1, 0))
    act_grad = input_grad(cotangent, second_kernel).astype(jnp.bfloat16)
    pre_grad = (act_grad.astype(jnp.float32) * silu_slope(first_pre)).astype(jnp.bfloat16)
    first_grad = kernel_grad(whole_input, pre_grad, (1, 0))
    flat = jnp.concatenate([first_grad.reshape(-1), second_grad.reshape(-1)])
    flat = lax.psum(flat, ("space", "sample"))
    first_grad = flat[: first_grad.size].reshape(first_grad.shape)
    second_grad = flat[first_grad.size :].reshape(second_grad.shape)
    return (features_out, first_grad, second_grad)


def solution(mesh):
    placed = (P("sample", None, "space", None), P(), P(), P(("sample", "space"), None, None, None))
    return jax.shard_map(
        body,
        mesh=mesh,
        in_specs=placed,
        out_specs=(P(("sample", "space"), None, None, None), P(), P()),
        check_vma=False,
    )
```

profile of v0, /device:TPU:1, one launch (start us, length us, event | category | flops | bytes accessed | tf_op | source)
XLA Modules:
  0.0 600.1 jit_solution(7680147417381081335)
XLA Ops:
  7.2 0.0 copy-start
  7.2 0.0 copy-start.3
  7.2 12.0 %all-to-all-start = ((bf16[32,16,2,1024]{3,2,1,0:T(2,128)(2,1)}), bf16[32,16,2,1024]{3,2,1,0:T(2,128)(2,1)S(1)}, u32[]{:S(2)}, u32[]{:S(2)}) async-start(bf16[32,16,2,1024]{3,2,1,0:T(2,128)(2,1)} %param.4), calls=%async_computation | async-start | bytes 4194304 | tf_op jit(solution)/shard_map/all_to_all | solution.py:53
  19.2 0.0 all-reduce.2.cloned.1.call-start
  19.3 1.2 copy.80
  20.5 0.2 copy.103
  20.7 0.1 pad.4.clone
  20.7 0.1 copy.83
  20.8 0.0 copy-done
  20.9 0.0 copy-done.3
  20.9 2.5 fusion.19
  23.3 5.4 copy.84
  28.7 38.9 %all-to-all-done = bf16[32,16,2,1024]{3,2,1,0:T(2,128)(2,1)S(1)} async-done(((bf16[32,16,2,1024]{3,2,1,0:T(2,128)(2,1)}), bf16[32,16,2,1024]{3,2,1,0:T(2,128)(2,1)S(1)}, u32[]{:S(2)}, u32[]{:S(2)}) %all-to-all-start) | async-done | bytes 2097184 | tf_op jit(solution)/shard_map/all_to_all | solution.py:53
  67.7 0.7 copy.68
  68.4 0.6 copy.104
  69.0 4.9 copy.102
  73.9 5.6 pad.clone
  79.5 0.0 copy-start.4
  79.5 0.0 copy-start.5
  79.5 32.4 %copy.71 = bf16[16,64,8,1,8,18]{0,4,5,2,1,3:T(8,128)(2,1)} copy(bf16[16,64,8,1,8,18]{1,2,5,4,0,3:T(8,128)(2,1)} %bitcast.50) | data formatting | bytes 4718592 | tf_op jit(solution)/shard_map/conv_general_dilated | solution.py:11
  111.9 3.9 slice.33
  115.8 0.0 copy-done.4
  115.8 0.0 copy-done.5
  115.8 20.2 %broadcast_select_fusion = (bf16[32,4,8,9,32]{4,2,3,1,0:T(8,128)(2,1)}, bf16[32,4,8,9,32]{4,2,3,1,0:T(8,128)(2,1)}, f32[32,4,8,9,32]{4,2,3,1,0:T(8,128)}) fusion(pred[8,9]{0,1:T(8,128)(4,1)S(1)} %copy-done.4, bf16[32,16,3,3,3]{0,1,4,3,2:T(8,128)(2,1)S(1)} %copy-done.5, bf16[16,64,8,1,7,2]{0,4,5,2,1,3:T(8,128)(2,1)} %slice.33, ...), kind=kOutput, calls=%fused_computation.30 | convolution fusion | flops 241065984 | bytes 4975688 | tf_op jit(solution)/shard_map/conv_general_dilated | solution.py:11
  136.0 2.6 copy.72
  138.6 0.0 copy-start.2
  138.6 0.4 slice.34
  139.1 1.4 copy.74
  140.4 0.0 copy-start.1
  140.4 1.0 fusion.48
  141.5 0.4 copy-done.1
  141.9 0.0 slice-start
  141.9 0.0 copy-done.2
  141.9 0.0 slice-start.1
  141.9 0.9 copy.89
  142.8 1.8 slice.40
  144.5 0.0 slice-done
  144.6 0.0 slice-done.1
  144.6 1.6 add_multiply_fusion
  146.2 4.8 copy.85
  151.0 11.8 %fusion.9 = f32[64,32,3,3,3]{0,1,4,3,2:T(8,128)S(1)} fusion(bf16[32,4,1,64,32]{4,0,3,1,2:T(8,128)(2,1)} %slice.40, bf16[1,64,16,2,32]{1,4,3,2,0:T(8,128)(2,1)S(1)} %bitcast.62), kind=kOutput, calls=%fused_computation.16 | convolution fusion | flops 91443200 | bytes 876544 | tf_op jit(solution)/shard_map/conv_general_dilated | solution.py:22
  162.9 12.3 %copy.93 = f32[64,32,3,3,3]{4,3,2,1,0:T(4,128)} copy(f32[64,32,3,3,3]{0,1,4,3,2:T(8,128)S(1)} %fusion.9) | data formatting | bytes 442368 | tf_op jit(solution)/shard_map/conv_general_dilated | solution.py:22
  175.2 11.0 %reshape.48 = f32[55296]{0:T(1024)} reshape(f32[64,32,3,3,3]{4,3,2,1,0:T(4,128)} %copy.93) | data formatting | bytes 442368 | tf_op jit(solution)/shard_map/reshape | solution.py:69
  186.1 34.9 %copy.86 = bf16[1,16,64,8,128]{1,0,4,3,2:T(2,128)(2,1)} copy(bf16[1,16,64,8,128]{4,3,1,2,0:T(8,128)(2,1)S(1)} %bitcast.49) | data formatting | bytes 4194304 | tf_op jit(solution)/shard_map/reshape | solution.py:54
  221.0 4.5 fusion.8
  225.5 89.8 %fusion.11 = f32[32,16,3,3,3]{0,1,4,3,2:T(8,128)} fusion(bf16[1,16,64,8,128]{1,0,4,3,2:T(2,128)(2,1)} %copy.86, bf16[32,4,1,64,32]{4,0,3,1,2:T(8,128)(2,1)S(1)} %fusion.8), kind=kOutput, calls=%fused_computation.18 | convolution fusion | flops 204385280 | bytes 2676736 | tf_op jit(solution)/shard_map/conv_general_dilated | solution.py:22
  315.3 4.4 copy.88
  319.7 2.0 reshape.47
  321.7 1.7 pad_maximum_fusion
  323.4 0.0 all-reduce.2.cloned.1.call-update
  323.4 3.5 fusion.26
  326.9 0.2 copy.77
  327.1 1.1 copy.94
  328.1 239.1 %all-reduce.2.cloned.1.call-done = f32[69120]{0:T(1024)} async-done(((f32[69120]{0:T(1024)}), f32[69120]{0:T(1024)}) %all-reduce.2.cloned.1.call-update) | async-done | bytes 276496 | tf_op jit(solution)/shard_map/psum | solution.py:70
  567.2 0.8 slice.41
  568.1 1.6 reshape.49
  569.6 2.5 copy.95
  572.1 1.0 slice.42
  573.1 8.3 %reshape.50 = f32[64,32,3,3,3]{4,3,2,1,0:T(4,128)} reshape(f32[55296]{0:T(1024)S(1)} %slice.42) | data formatting | bytes 442368 | tf_op jit(solution)/shard_map/reshape | solution.py:72
  581.4 11.7 %copy.96 = f32[64,32,3,3,3]{0,1,4,3,2:T(8,128)} copy(f32[64,32,3,3,3]{4,3,2,1,0:T(4,128)} %reshape.50) | data formatting | bytes 442368
  (2 shorter events, 0.0 us)
Async XLA Ops:
  7.2 13.7 %copy-start = (bf16[64,32,3,3,3]{0,1,4,3,2:T(8,128)(2,1)S(1)}, bf16[64,32,3,3,3]{0,1,4,3,2:T(8,128)(2,1)}, u32[]{:S(2)}) copy-start(bf16[64,32,3,3,3]{0,1,4,3,2:T(8,128)(2,1)} %param.6) | copy-start | bytes 331780
  7.2 13.7 %copy-start.3 = (pred[8,10]{0,1:T(8,128)(4,1)S(1)}, pred[8,10]{0,1:T(8,128)(4,1)}, u32[]{:S(2)}) copy-start(pred[8,10]{0,1:T(8,128)(4,1)} %constant.19) | copy-start | bytes 244
  7.2 60.5 %all-to-all-start = ((bf16[32,16,2,1024]{3,2,1,0:T(2,128)(2,1)}), bf16[32,16,2,1024]{3,2,1,0:T(2,128)(2,1)S(1)}, u32[]{:S(2)}, u32[]{:S(2)}) async-start(bf16[32,16,2,1024]{3,2,1,0:T(2,128)(2,1)} %param.4), calls=%async_computation | async-start | bytes 4194304 | tf_op jit(solution)/shard_map/all_to_all | solution.py:53
  19.2 548.0 %all-reduce.2.cloned.1.call-start = ((), (), s32[]{:S(2)}) async-start(), calls=%async_computation.1 | async-start | bytes 557056 | tf_op jit(solution)/shard_map/psum | solution.py:70
  79.5 36.3 %copy-start.4 = (pred[8,9]{0,1:T(8,128)(4,1)S(1)}, pred[8,9]{0,1:T(8,128)(4,1)}, u32[]{:S(2)}) copy-start(pred[8,9]{0,1:T(8,128)(4,1)} %constant.17) | copy-start | bytes 220
  79.5 36.3 %copy-start.5 = (bf16[32,16,3,3,3]{0,1,4,3,2:T(8,128)(2,1)S(1)}, bf16[32,16,3,3,3]{0,1,4,3,2:T(8,128)(2,1)}, u32[]{:S(2)}) copy-start(bf16[32,16,3,3,3]{0,1,4,3,2:T(8,128)(2,1)} %param.5) | copy-start | bytes 82948
  138.6 3.3 copy-start.2
  140.4 1.5 copy-start.1
  141.9 2.7 slice-start
  141.9 2.7 slice-start.1
Sparse Core Ops, SparseCore 0:
  323.5 243.6 all-reduce.1
where the time goes:
time: 607 us; the launch traced here: 600 us
  waiting for transfers between devices  278 us (46%)
  local copies, waits for them, and re-layouts  160 us (26%)
  matrix products  128 us (21%)
  between operations  14.4 us (2%)
  starting transfers between devices  12.1 us (2%)
  other arithmetic  7.78 us (1%)
    psum x1, waiting for transfers between devices, body(): flat = lax.psum(flat, ('space', 'sample'))  239 us
    conv_general_dilated x2, matrix products, kernel_grad(): lax.conv_general_dilated(field, cotangent, (1, 1, 1), (depth_pad, (1, 0),...  102 us
    reshape x2, local copies, waits for them, and re-layouts, body(): whole_input.reshape(whole_input.shape[0], channels_in, whole_input.shape[...  40.5 us
    all_to_all x1, waiting for transfers between devices, body(): lax.all_to_all(crops, 'space', split_axis=0, concat_axis=2, tiled=True)  38.9 us
    conv_general_dilated x2, local copies, waits for them, and re-layouts, forward_conv(): lax.conv_general_dilated(field, kernel, (2, 2, 2), (depth_pad, (1, 0), (1...  36.3 us
    conv_general_dilated x2, matrix products, forward_conv(): lax.conv_general_dilated(field, kernel, (2, 2, 2), (depth_pad, (1, 0), (1...  23.7 us
    unnamed x23, local copies, waits for them, and re-layouts  22.7 us
    conv_general_dilated x2, local copies, waits for them, and re-layouts, kernel_grad(): lax.conv_general_dilated(field, cotangent, (1, 1, 1), (depth_pad, (1, 0),...  16.7 us
  transfers between devices with their start and end apart: 2, of which 2 were waited for; matrix products, arithmetic and copies ran while one was open for 2% of the time, Pallas kernels for 0%

commit v1 on v0

--- a/solution.py
+++ b/solution.py
@@ -67,7 +67,7 @@
     pre_grad = (act_grad.astype(jnp.float32) * silu_slope(first_pre)).astype(jnp.bfloat16)
     first_grad = kernel_grad(whole_input, pre_grad, (1, 0))
     flat = jnp.concatenate([first_grad.reshape(-1), second_grad.reshape(-1)])
-    flat = lax.psum(flat, ("space", "sample"))
+    flat = lax.psum(lax.psum(flat, "sample"), "space")
     first_grad = flat[: first_grad.size].reshape(first_grad.shape)
     second_grad = flat[first_grad.size :].reshape(second_grad.shape)
     return (features_out, first_grad, second_grad)

time: 607 us -> 574 us (0.946)
  waiting for transfers between devices: 278 us -> 240 us
    psum x1 -> x2, waiting for transfers between devices: 239 us -> 201 us  [body(): flat = lax.psum(lax.psum(flat, 'sample'), 'space')]
    unnamed x23 -> x21, local copies, waits for them, and re-layouts: 22.7 us -> 22.3 us
  transfers between devices with their start and end apart: 2 -> 3, of which waited for: 2 -> 3; matrix products, arithmetic and copies ran while one was open for 2% -> 3% of each run, Pallas kernels for 0% -> 0%
where the time goes in v1:
time: 574 us; the launch traced here: 564 us
  waiting for transfers between devices  240 us (42%)
  local copies, waits for them, and re-layouts  162 us (28%)
  matrix products  127 us (22%)
  between operations  14.5 us (3%)
  starting transfers between devices  12.1 us (2%)
  other arithmetic  7.78 us (1%)
    psum x2, waiting for transfers between devices, body(): flat = lax.psum(lax.psum(flat, 'sample'), 'space')  201 us
    conv_general_dilated x2, matrix products, kernel_grad(): lax.conv_general_dilated(field, cotangent, (1, 1, 1), (depth_pad, (1, 0),...  102 us
    reshape x2, local copies, waits for them, and re-layouts, body(): whole_input.reshape(whole_input.shape[0], channels_in, whole_input.shape[...  40.6 us
    all_to_all x1, waiting for transfers between devices, body(): lax.all_to_all(crops, 'space', split_axis=0, concat_axis=2, tiled=True)  38.9 us
    conv_general_dilated x2, local copies, waits for them, and re-layouts, forward_conv(): lax.conv_general_dilated(field, kernel, (2, 2, 2), (depth_pad, (1, 0), (1...  36.3 us
    conv_general_dilated x2, matrix products, forward_conv(): lax.conv_general_dilated(field, kernel, (2, 2, 2), (depth_pad, (1, 0), (1...  23.5 us
    unnamed x21, local copies, waits for them, and re-layouts  22.3 us
    conv_general_dilated x2, local copies, waits for them, and re-layouts, kernel_grad(): lax.conv_general_dilated(field, cotangent, (1, 1, 1), (depth_pad, (1, 0),...  16.8 us
  transfers between devices with their start and end apart: 3, of which 3 were waited for; matrix products, arithmetic and copies ran while one was open for 3% of the time, Pallas kernels for 0%

profile of v1, /device:TPU:1, one launch (start us, length us, event | category | flops | bytes accessed | tf_op | source)
XLA Modules:
  0.0 563.8 jit_solution(12953845877035143694)
XLA Ops:
  7.2 0.0 copy-start
  7.2 0.0 copy-start.2
  7.2 12.0 %all-to-all-start = ((bf16[32,16,2,1024]{3,2,1,0:T(2,128)(2,1)}), bf16[32,16,2,1024]{3,2,1,0:T(2,128)(2,1)S(1)}, u32[]{:S(2)}, u32[]{:S(2)}) async-start(bf16[32,16,2,1024]{3,2,1,0:T(2,128)(2,1)} %param.4), calls=%async_computation | async-start | bytes 4194304 | tf_op jit(solution)/shard_map/all_to_all | solution.py:53
  19.2 0.0 all-reduce.3.cloned.1.call-start
  19.3 1.2 copy.80
  20.5 0.2 copy.103
  20.7 0.1 pad.4.clone
  20.7 0.1 copy.83
  20.8 0.0 copy-done
  20.9 0.0 copy-done.2
  20.9 2.4 fusion.19
  23.3 5.4 copy.84
  28.7 38.9 %all-to-all-done = bf16[32,16,2,1024]{3,2,1,0:T(2,128)(2,1)S(1)} async-done(((bf16[32,16,2,1024]{3,2,1,0:T(2,128)(2,1)}), bf16[32,16,2,1024]{3,2,1,0:T(2,128)(2,1)S(1)}, u32[]{:S(2)}, u32[]{:S(2)}) %all-to-all-start) | async-done | bytes 2097184 | tf_op jit(solution)/shard_map/all_to_all | solution.py:53
  67.7 0.7 copy.68
  68.4 0.6 copy.104
  69.0 4.9 copy.102
  73.9 5.6 pad.clone
  79.5 0.0 copy-start.3
  79.6 0.0 copy-start.4
  79.6 32.5 %copy.71 = bf16[16,64,8,1,8,18]{0,4,5,2,1,3:T(8,128)(2,1)} copy(bf16[16,64,8,1,8,18]{1,2,5,4,0,3:T(8,128)(2,1)} %bitcast.50) | data formatting | bytes 4718592 | tf_op jit(solution)/shard_map/conv_general_dilated | solution.py:11
  112.0 3.9 slice.33
  115.9 0.0 copy-done.3
  115.9 0.0 copy-done.4
  115.9 20.2 %broadcast_select_fusion = (bf16[32,4,8,9,32]{4,2,3,1,0:T(8,128)(2,1)}, bf16[32,4,8,9,32]{4,2,3,1,0:T(8,128)(2,1)}, f32[32,4,8,9,32]{4,2,3,1,0:T(8,128)}) fusion(pred[8,9]{0,1:T(8,128)(4,1)S(1)} %copy-done.3, bf16[32,16,3,3,3]{0,1,4,3,2:T(8,128)(2,1)S(1)} %copy-done.4, bf16[16,64,8,1,7,2]{0,4,5,2,1,3:T(8,128)(2,1)} %slice.33, ...), kind=kOutput, calls=%fused_computation.30 | convolution fusion | flops 241065984 | bytes 4975688 | tf_op jit(solution)/shard_map/conv_general_dilated | solution.py:11
  136.1 2.6 copy.72
  138.6 0.0 copy-start.1
  138.7 0.4 slice.34
  139.1 2.6 copy.74
  141.7 0.0 slice-start
  141.7 0.0 copy-done.1
  141.7 0.0 slice-start.1
  141.8 0.9 copy.89
  142.7 1.8 slice.40
  144.4 0.0 slice-done
  144.4 0.0 slice-done.1
  144.4 1.6 add_multiply_fusion
  146.0 4.9 copy.85
  150.9 11.8 %fusion.9 = f32[64,32,3,3,3]{0,1,4,3,2:T(8,128)S(1)} fusion(bf16[32,4,1,64,32]{4,0,3,1,2:T(8,128)(2,1)} %slice.40, bf16[1,64,16,2,32]{1,4,3,2,0:T(8,128)(2,1)S(1)} %bitcast.62), kind=kOutput, calls=%fused_computation.16 | convolution fusion | flops 91443200 | bytes 876544 | tf_op jit(solution)/shard_map/conv_general_dilated | solution.py:22
  162.7 12.4 %copy.93 = f32[64,32,3,3,3]{4,3,2,1,0:T(4,128)} copy(f32[64,32,3,3,3]{0,1,4,3,2:T(8,128)S(1)} %fusion.9) | data formatting | bytes 442368 | tf_op jit(solution)/shard_map/conv_general_dilated | solution.py:22
  175.2 11.0 %reshape.48 = f32[55296]{0:T(1024)} reshape(f32[64,32,3,3,3]{4,3,2,1,0:T(4,128)} %copy.93) | data formatting | bytes 442368 | tf_op jit(solution)/shard_map/reshape | solution.py:69
  186.1 35.0 %copy.86 = bf16[1,16,64,8,128]{1,0,4,3,2:T(2,128)(2,1)} copy(bf16[1,16,64,8,128]{4,3,1,2,0:T(8,128)(2,1)S(1)} %bitcast.49) | data formatting | bytes 4194304 | tf_op jit(solution)/shard_map/reshape | solution.py:54
  221.1 4.5 fusion.8
  225.6 89.8 %fusion.11 = f32[32,16,3,3,3]{0,1,4,3,2:T(8,128)} fusion(bf16[1,16,64,8,128]{1,0,4,3,2:T(2,128)(2,1)} %copy.86, bf16[32,4,1,64,32]{4,0,3,1,2:T(8,128)(2,1)S(1)} %fusion.8), kind=kOutput, calls=%fused_computation.18 | convolution fusion | flops 204385280 | bytes 2676736 | tf_op jit(solution)/shard_map/conv_general_dilated | solution.py:22
  315.4 4.4 copy.88
  319.8 2.0 reshape.47
  321.8 1.7 pad_maximum_fusion
  323.4 0.0 all-reduce.3.cloned.1.call-update
  323.5 0.0 all-reduce.5.cloned.1.call-start
  323.5 1.1 fusion.48
  324.6 61.6 %all-reduce.3.cloned.1.call-done = f32[69120]{0:T(1024)} async-done(((f32[69120]{0:T(1024)}), f32[69120]{0:T(1024)}) %all-reduce.3.cloned.1.call-update) | async-done | bytes 276496 | tf_op jit(solution)/shard_map/psum | solution.py:70
  386.3 0.0 all-reduce.5.cloned.1.call-update
  386.3 3.3 fusion.26
  389.6 0.2 copy.77
  389.8 1.1 copy.94
  390.8 139.8 %all-reduce.5.cloned.1.call-done = f32[69120]{0:T(1024)} async-done(((f32[69120]{0:T(1024)}), f32[69120]{0:T(1024)}) %all-reduce.5.cloned.1.call-update) | async-done | bytes 276496 | tf_op jit(solution)/shard_map/psum | solution.py:70
  530.7 0.8 slice.41
  531.5 1.8 reshape.49
  533.3 2.5 copy.95
  535.8 1.0 slice.42
  536.7 8.3 %reshape.50 = f32[64,32,3,3,3]{4,3,2,1,0:T(4,128)} reshape(f32[55296]{0:T(1024)S(1)} %slice.42) | data formatting | bytes 442368 | tf_op jit(solution)/shard_map/reshape | solution.py:72
  545.1 11.7 %copy.96 = f32[64,32,3,3,3]{0,1,4,3,2:T(8,128)} copy(f32[64,32,3,3,3]{4,3,2,1,0:T(4,128)} %reshape.50) | data formatting | bytes 442368
  (2 shorter events, 0.0 us)
Async XLA Ops:
  7.2 13.7 %copy-start = (bf16[64,32,3,3,3]{0,1,4,3,2:T(8,128)(2,1)S(1)}, bf16[64,32,3,3,3]{0,1,4,3,2:T(8,128)(2,1)}, u32[]{:S(2)}) copy-start(bf16[64,32,3,3,3]{0,1,4,3,2:T(8,128)(2,1)} %param.6) | copy-start | bytes 331780
  7.2 13.7 %copy-start.2 = (pred[8,10]{0,1:T(8,128)(4,1)S(1)}, pred[8,10]{0,1:T(8,128)(4,1)}, u32[]{:S(2)}) copy-start(pred[8,10]{0,1:T(8,128)(4,1)} %constant.19) | copy-start | bytes 244
  7.2 60.5 %all-to-all-start = ((bf16[32,16,2,1024]{3,2,1,0:T(2,128)(2,1)}), bf16[32,16,2,1024]{3,2,1,0:T(2,128)(2,1)S(1)}, u32[]{:S(2)}, u32[]{:S(2)}) async-start(bf16[32,16,2,1024]{3,2,1,0:T(2,128)(2,1)} %param.4), calls=%async_computation | async-start | bytes 4194304 | tf_op jit(solution)/shard_map/all_to_all | solution.py:53
  19.2 367.1 %all-reduce.3.cloned.1.call-start = ((), (), s32[]{:S(2)}) async-start(), calls=%async_computation.1 | async-start | bytes 557056 | tf_op jit(solution)/shard_map/psum | solution.py:70
  79.5 36.3 %copy-start.3 = (pred[8,9]{0,1:T(8,128)(4,1)S(1)}, pred[8,9]{0,1:T(8,128)(4,1)}, u32[]{:S(2)}) copy-start(pred[8,9]{0,1:T(8,128)(4,1)} %constant.17) | copy-start | bytes 220
  79.6 36.3 %copy-start.4 = (bf16[32,16,3,3,3]{0,1,4,3,2:T(8,128)(2,1)S(1)}, bf16[32,16,3,3,3]{0,1,4,3,2:T(8,128)(2,1)}, u32[]{:S(2)}) copy-start(bf16[32,16,3,3,3]{0,1,4,3,2:T(8,128)(2,1)} %param.5) | copy-start | bytes 82948
  138.6 3.1 copy-start.1
  141.7 2.7 slice-start
  141.7 2.7 slice-start.1
  323.5 207.2 %all-reduce.5.cloned.1.call-start = ((), (), s32[]{:S(2)}) async-start(), calls=%async_computation.2 | async-start | bytes 557056 | tf_op jit(solution)/shard_map/psum | solution.py:70
Sparse Core Ops, SparseCore 0:
  323.6 62.6 all-reduce.2
  390.1 140.5 all-reduce.4
